TPU v7x, 32 devices: a whole 2x2x4 slice. The times are simulated.
32 devices in a mesh: rows: 8 (over z, y), vecs: 4 (over x, core).
Axes of the slice: x: 2, y: 2, z: 4, core: 2. Of those that a mesh axis runs over, the one named last changes fastest.
Arguments:
- vectors: bfloat16 [24576, 512], P('rows', 'vecs'), may hold values from -8 to 8
- node_mass: float32 [24576], P('rows'), may hold values from 0.5 to 2
- cable_stiff: float32 [24576], P('rows'), may hold values from 0.1 to 1
- cable_nodes: int32 [8, 4], P('rows'), may hold values from 1 to 1152, 2304 in all within a row
- deck_rigidity: float32 [], replicated, may hold values from 0.3 to 1
- anchor_rows: int32 [8, 8, 4], P('rows'), may hold values from 0 to 3072, as said below
- anchor_stiff: float32 [8, 8, 4], P('rows'), may hold values from 0.2 to 1, as said below
- cut_low: float32 [], replicated, may hold values from 1.5 to 2.5
- top_bound: float32 [], replicated, may hold values from 7 to 9
Outputs:
- basis: bfloat16 [24576, 512], P('rows', 'vecs')
Inputs may be any that keep to these rules, and one draw needn't show every extreme that they name: anchor_rows[r, q, s] is a node of partition r coupled through slot s to partition q, or 3072 where the slot is empty; slot s of r towards q is live exactly when slot s of q towards r is; live slots come first; no partition has live slots towards itself; a partition that is not a pylon partition has live slots only towards the partitions beside it in the cyclic order, which fill all 4 slots, and towards at most 4 pylon partitions; pylon partitions come in pairs half the cyclic order apart, and the two of a pair fill all 4 slots towards each other. anchor_stiff[r, q, s] equals anchor_stiff[q, r, s].
All inputs are finite; a program needn't handle non-finite values.
Results may differ from a plain program's by a relative error of at most 0.0072.
The roundings to bfloat16 on the way count: a program that leaves them out, or rounds other values in their place, can miss the bound.
Values may be sent and summed in bfloat16 or wider, within the bound.
A program may use at most 64 MiB of HBM per device.

v0:
```python
import jax
import jax.numpy as jnp
from jax import lax
from jax.sharding import PartitionSpec as P

CABLE_ROWS = 2304


def with_halo(block, sides, width):
    for axis, dim in sides:
        count = lax.axis_size(axis)
        forward = [(i, i + 1) for i in range(count - 1)]
        backward = [(target, source) for source, target in forward]
        low = lax.ppermute(
            lax.slice_in_dim(block, block.shape[dim] - width, None, axis=dim), axis, forward
        )
        high = lax.ppermute(lax.slice_in_dim(block, 0, width, axis=dim), axis, backward)
        block = jnp.concatenate([low, block, high], axis=dim)
    return block


def body(
    vectors,
    node_mass,
    cable_stiff,
    cable_nodes,
    deck_rigidity,
    anchor_rows,
    anchor_stiff,
    cut_low,
    top_bound,
):
    part_count = lax.axis_size("rows")
    my_index = lax.axis_index("rows")
    own_width = vectors.shape[1]
    cable_ends = jnp.cumsum(cable_nodes[0])
    positions = jnp.arange(CABLE_ROWS - 1, dtype=jnp.int32) + 1
    breaks = jnp.any(positions[:, None] == cable_ends[None, :], axis=1)
    cable_links = jnp.where(breaks, 0.0, cable_stiff[: CABLE_ROWS - 1])[:, None]
    left_open = jnp.where(my_index > 0, deck_rigidity, 0.0)
    right_open = jnp.where(my_index < part_count - 1, deck_rigidity, 0.0)
    slot_rows = anchor_rows[0]
    slot_stiff = anchor_stiff[0][:, :, None]
    flat_rows = slot_rows.reshape(-1)

    def apply_operator(values):
        cable_part = values[:CABLE_ROWS]
        deck_part = values[CABLE_ROWS:]
        cable_flux = cable_links * (cable_part[:-1] - cable_part[1:])
        cable_side = jnp.pad(cable_flux, ((0, 1), (0, 0))) - jnp.pad(cable_flux, ((1, 0), (0, 0)))
        outgoing = jnp.take(values, slot_rows, axis=0, mode="fill", fill_value=0.0)
        incoming = lax.all_to_all(
            outgoing.astype(jnp.bfloat16), "rows", split_axis=0, concat_axis=0, tiled=True
        ).astype(outgoing.dtype)
        padded = with_halo(deck_part.astype(jnp.bfloat16), (("rows", 0),), 1).astype(
            deck_part.dtype
        )
        before_row = padded[0]
        after_row = padded[-1]
        deck_flux = deck_rigidity * (deck_part[:-1] - deck_part[1:])
        first_flux = left_open * (before_row - deck_part[0])
        last_flux = right_open * (deck_part[-1] - after_row)
        deck_side = jnp.concatenate([deck_flux, last_flux[None, :]], axis=0) - jnp.concatenate(
            [first_flux[None, :], deck_flux], axis=0
        )
        anchor_force = (slot_stiff * (outgoing - incoming)).reshape(-1, values.shape[1])
        anchor_side = jnp.zeros_like(values).at[flat_rows].add(anchor_force, mode="drop")
        springs = jnp.concatenate([cable_side, deck_side], axis=0)
        return node_mass[:, None] * values + springs + anchor_side

    start_block = vectors.astype(jnp.float32)
    center = (top_bound + cut_low) * 0.5
    half_width = (top_bound - cut_low) * 0.5
    first_degree = (apply_operator(start_block) - center * start_block) / half_width
    second_degree = (
        2.0 * (apply_operator(first_degree) - center * first_degree) / half_width - start_block
    )
    filtered = second_degree.astype(jnp.bfloat16)
    columns = lax.all_gather(filtered, "vecs", axis=1, tiled=True)
    total_rows = filtered.shape[0] * part_count
    gram_whole = jnp.einsum("rb,rc->bc", columns, columns, preferred_element_type=jnp.float32)
    gram_matrix = lax.psum(gram_whole, "rows") / total_rows
    lower_factor = jnp.linalg.cholesky(gram_matrix)
    identity = jnp.eye(gram_matrix.shape[0], dtype=jnp.float32)
    inverse = jax.scipy.linalg.solve_triangular(lower_factor, identity, lower=True)
    factor = inverse.T.astype(jnp.bfloat16)
    own_factor = lax.dynamic_slice_in_dim(factor, lax.axis_index("vecs") * own_width, own_width, 1)
    return jnp.dot(columns, own_factor, preferred_element_type=jnp.float32).astype(jnp.bfloat16)


def solution(mesh):
    return jax.shard_map(
        body,
        mesh=mesh,
        in_specs=(
            P("rows", "vecs"),
            P("rows"),
            P("rows"),
            P("rows", None),
            P(),
            P("rows", None, None),
            P("rows", None, None),
            P(),
            P(),
        ),
        out_specs=P("rows", "vecs"),
        check_vma=False,
    )
```

profile of v0, /device:TPU:0, one launch (start us, length us, event | category | flops | bytes accessed | tf_op | source)
XLA Modules:
  0.0 327.3 jit_solution(2909291328228950229)
XLA Ops:
  6.5 0.7 fusion.50
  7.3 1.3 collective-permute-start.1
  8.6 5.5 %collective-permute-start = (bf16[1,128]{1,0:T(2,128)(2,1)S(1)}, bf16[1,128]{1,0:T(2,128)(2,1)S(1)}, u32[]{:S(2)}, u32[]{:S(2)}) collective-permute-start(bf16[1,128]{1,0:T(2,128)(2,1)S(1)} %get-tuple-element.32), channel_id=1, source_target_pairs={{0,4},{4,8},{8,12},{12,16},{16,20},{20,24},{24,28},{1,5},{5,9},{9,... | collective-permute-start | bytes 776 | tf_op jit(solution)/shard_map/ppermute | solution.py:14
  14.1 1.2 convert_element_type.44
  15.6 0.6 gather_fusion
  16.2 0.7 select_convert_fusion.1
  16.9 6.2 %all-to-all-start = ((bf16[8,4,128]{2,1,0:T(4,128)(2,1)}), bf16[8,4,128]{2,1,0:T(4,128)(2,1)S(1)}, u32[]{:S(2)}, u32[]{:S(2)}) async-start(bf16[8,4,128]{2,1,0:T(4,128)(2,1)} %select_convert_fusion.1), calls=%async_computation | async-start | bytes 16384 | tf_op jit(solution)/shard_map/all_to_all | solution.py:52
  25.6 0.4 fusion.1
  26.0 1.1 pad_subtract_fusion.1
  27.6 2.9 maximum_add_fusion
  30.6 3.3 scatter_fusion
  33.9 2.5 fusion.47
  36.5 1.4 fusion
  37.9 0.6 gather_fusion.1
  38.4 0.7 fusion.49
  39.2 1.3 collective-permute-start.3
  40.4 4.6 %collective-permute-start.2 = (bf16[1,128]{1,0:T(2,128)(2,1)S(1)}, bf16[1,128]{1,0:T(2,128)(2,1)S(1)}, u32[]{:S(2)}, u32[]{:S(2)}) collective-permute-start(bf16[1,128]{1,0:T(2,128)(2,1)S(1)} %get-tuple-element.30), channel_id=1, source_target_pairs={{0,4},{4,8},{8,12},{12,16},{16,20},{20,24},{24,28},{1,5},{5,9},{9,... | collective-permute-start | bytes 776 | tf_op jit(solution)/shard_map/ppermute | solution.py:14
  45.0 2.8 pad_subtract_fusion
  47.8 0.7 select_convert_fusion
  48.4 0.9 slice.253
  49.4 6.0 %all-to-all-start.1 = ((bf16[8,4,128]{2,1,0:T(4,128)(2,1)}), bf16[8,4,128]{2,1,0:T(4,128)(2,1)S(1)}, u32[]{:S(2)}, u32[]{:S(2)}) async-start(bf16[8,4,128]{2,1,0:T(4,128)(2,1)} %select_convert_fusion), calls=%async_computation.1 | async-start | bytes 16384 | tf_op jit(solution)/shard_map/all_to_all | solution.py:52
  55.5 2.9 maximum_add_fusion.1
  58.4 3.5 %all-to-all-done.1 = bf16[8,4,128]{2,1,0:T(4,128)(2,1)S(1)} async-done(((bf16[8,4,128]{2,1,0:T(4,128)(2,1)}), bf16[8,4,128]{2,1,0:T(4,128)(2,1)S(1)}, u32[]{:S(2)}, u32[]{:S(2)}) %all-to-all-start.1) | async-done | bytes 8224 | tf_op jit(solution)/shard_map/all_to_all | solution.py:52
  62.0 3.3 scatter_fusion.1
  65.3 2.6 subtract_convert_fusion
  67.9 0.5 all-reduce.7.cloned.1.call-start
  68.4 26.4 %all-gather.2.cloned.1.call-done = bf16[3072,512]{1,0:T(8,128)(2,1)} async-done(((bf16[3072,128]{1,0:T(8,128)(2,1)}), bf16[3072,512]{1,0:T(8,128)(2,1)}) %all-gather.2.cloned.1.call-update) | async-done | bytes 3145744 | tf_op jit(solution)/shard_map/all_gather | solution.py:79
  94.9 5.7 %fusion.54 = f32[512,512]{0,1:T(8,128)} fusion(bf16[3072,512]{1,0:T(8,128)(2,1)} %all-gather.2.cloned.1.call-done), kind=kOutput, calls=%fused_computation.131 | convolution fusion | flops 1610612736 | bytes 4194304 | tf_op jit(solution)/shard_map/rb,rc->bc/dot_general | solution.py:81
  100.7 1.1 fusion.13
  101.8 77.2 %all-reduce.7.cloned.1.call-done = f32[512,512]{0,1:T(8,128)} async-done(((f32[512,512]{0,1:T(8,128)}), f32[512,512]{0,1:T(8,128)}) %all-reduce.7.cloned.1.call-update) | async-done | bytes 1048592 | tf_op jit(solution)/shard_map/psum | solution.py:82
  179.0 1.3 broadcast_multiply_fusion
  180.3 0.3 copy.33
  180.6 0.9 copy-done.2
  181.8 11.7 %cholesky.104 = f32[128,128]{1,0:T(8,128)S(1)} custom-call(f32[128,128]{1,0:T(8,128)S(1)} %cholesky.266), custom_call_target="Cholesky" | custom-call | tf_op jit(solution)/shard_map/jit(cholesky)/cholesky | solution.py:83
  193.7 9.8 %custom-call.31 = f32[1,128,128]{1,2,0:T(8,128)S(1)} custom-call(f32[1,128,128]{2,1,0:T(8,128)S(1)} %get-tuple-element.43), custom_call_target="InvertDiagBlocksLowerTriangular" | custom-call | tf_op jit(solution)/shard_map/jit(cholesky)/cholesky | solution.py:83
  203.8 0.3 convolution_subtract_fusion.3
  204.1 11.9 %cholesky.217 = f32[128,128]{1,0:T(8,128)S(1)} custom-call(f32[128,128]{1,0:T(8,128)S(1)} %cholesky.270), custom_call_target="Cholesky" | custom-call | tf_op jit(solution)/shard_map/jit(cholesky)/cholesky | solution.py:83
  216.0 9.8 %custom-call.32 = f32[1,128,128]{1,2,0:T(8,128)S(1)} custom-call(f32[1,128,128]{2,1,0:T(8,128)S(1)} %get-tuple-element.40), custom_call_target="InvertDiagBlocksLowerTriangular" | custom-call | tf_op jit(solution)/shard_map/jit(cholesky)/cholesky | solution.py:83
  226.1 0.4 convolution_subtract_fusion.4
  226.5 11.7 %cholesky.238 = f32[128,128]{1,0:T(8,128)S(1)} custom-call(f32[128,128]{1,0:T(8,128)S(1)} %cholesky.275), custom_call_target="Cholesky" | custom-call | tf_op jit(solution)/shard_map/jit(cholesky)/cholesky | solution.py:83
  238.3 9.8 %custom-call.33 = f32[1,128,128]{1,2,0:T(8,128)S(1)} custom-call(f32[1,128,128]{2,1,0:T(8,128)S(1)} %get-tuple-element.37), custom_call_target="InvertDiagBlocksLowerTriangular" | custom-call | tf_op jit(solution)/shard_map/jit(cholesky)/cholesky | solution.py:83
  248.3 0.4 convolution_subtract_fusion.5
  248.7 11.9 %cholesky.255 = f32[128,128]{1,0:T(8,128)S(1)} custom-call(f32[128,128]{1,0:T(8,128)S(1)} %convolution_subtract_fusion.5), custom_call_target="Cholesky" | custom-call | tf_op jit(solution)/shard_map/jit(cholesky)/cholesky | solution.py:83
  260.6 0.6 compare_reduce_fusion.2
  261.3 0.6 compare_reduce_fusion.1
  261.9 0.7 compare_reduce_fusion.3
  265.1 9.7 %while.1 = (s32[]{:T(128)}, f32[512,512]{1,0:T(8,128)S(1)}, s32[4,2]{0,1:T(2,128)S(1)}, f32[4,128,128]{2,1,0:T(8,128)}, s32[]{:T(128)}) while((s32[]{:T(128)}, f32[512,512]{1,0:T(8,128)S(1)}, s32[4,2]{0,1:T(2,128)S(1)}, f32[4,128,128]{2,1,0:T(8,128)}, s32[]{:T(128)}) %tuple.36), condition=%wide.while_cond, body=%wide.while_body.sunk | while | flops 2 | bytes 132205 | solution.py:85
  265.2 0.5 fusion.64
  265.7 1.8 bitcast_dynamic-update-slice_fusion.2
  267.7 0.5 fusion.64
  268.2 1.8 bitcast_dynamic-update-slice_fusion.2
  270.1 0.5 fusion.64
  270.6 1.8 bitcast_dynamic-update-slice_fusion.2
  272.5 0.5 fusion.64
  273.0 1.8 bitcast_dynamic-update-slice_fusion.2
  274.9 40.1 %custom-call.34 = f32[4,128,128]{1,2,0:T(8,128)S(1)} custom-call(f32[4,128,128]{2,1,0:T(8,128)} %get-tuple-element.13), custom_call_target="InvertDiagBlocksLowerTriangular" | custom-call | tf_op jit(solution)/shard_map/jit(_solve_triangular)/triangular_solve | solution.py:85
  315.0 0.3 fusion.51
  315.4 0.4 convolution_subtract_fusion.1
  315.7 0.4 fusion.52
  316.2 0.4 convolution_subtract_fusion
  316.6 0.4 fusion.53
  317.0 0.6 convolution_subtract_fusion.2
  317.7 0.4 convolution_convert_fusion.1
  318.1 2.1 convolution_convert_fusion
  (70 shorter events, 3.4 us)
Async XLA Ops:
  6.5 8.8 %copy-start.5 = (s32[1,8,4]{1,2,0:T(4,128)S(1)}, s32[1,8,4]{1,2,0:T(4,128)}, u32[]{:S(2)}) copy-start(s32[1,8,4]{1,2,0:T(4,128)} %param.16) | copy-start | bytes 388
  7.3 20.0 %collective-permute-start.1 = (bf16[1,128]{1,0:T(2,128)(2,1)S(1)}, bf16[1,128]{1,0:T(2,128)(2,1)S(1)}, u32[]{:S(2)}, u32[]{:S(2)}) collective-permute-start(bf16[1,128]{1,0:T(2,128)(2,1)S(1)} %get-tuple-element.33), channel_id=1, source_target_pairs={{4,0},{8,4},{12,8},{16,12},{20,16},{24,20},{28,24},{5,1},{9,5},{13... | collective-permute-start | bytes 776 | tf_op jit(solution)/shard_map/ppermute | solution.py:17
  8.5 16.7 %copy-start.8 = (s32[1,4]{1,0:T(1,128)S(1)}, s32[1,4]{1,0:T(1,128)}, u32[]{:S(2)}) copy-start(s32[1,4]{1,0:T(1,128)} %param.14) | copy-start | bytes 52
  8.6 17.0 %copy-start.6 = (f32[3072]{0:T(1024)S(1)}, f32[3072]{0:T(1024)}, u32[]{:S(2)}) copy-start(f32[3072]{0:T(1024)} %param.13) | copy-start | bytes 36868
  8.6 18.7 %collective-permute-start = (bf16[1,128]{1,0:T(2,128)(2,1)S(1)}, bf16[1,128]{1,0:T(2,128)(2,1)S(1)}, u32[]{:S(2)}, u32[]{:S(2)}) collective-permute-start(bf16[1,128]{1,0:T(2,128)(2,1)S(1)} %get-tuple-element.32), channel_id=1, source_target_pairs={{0,4},{4,8},{8,12},{12,16},{16,20},{20,24},{24,28},{1,5},{5,9},{9,... | collective-permute-start | bytes 776 | tf_op jit(solution)/shard_map/ppermute | solution.py:14
  16.9 13.6 %all-to-all-start = ((bf16[8,4,128]{2,1,0:T(4,128)(2,1)}), bf16[8,4,128]{2,1,0:T(4,128)(2,1)S(1)}, u32[]{:S(2)}, u32[]{:S(2)}) async-start(bf16[8,4,128]{2,1,0:T(4,128)(2,1)} %select_convert_fusion.1), calls=%async_computation | async-start | bytes 16384 | tf_op jit(solution)/shard_map/all_to_all | solution.py:52
  25.9 1.3 copy-start.7
  25.9 1.4 slice-start
  26.0 1.6 copy-start
  26.0 1.6 copy-start.4
  39.2 16.3 %collective-permute-start.3 = (bf16[1,128]{1,0:T(2,128)(2,1)S(1)}, bf16[1,128]{1,0:T(2,128)(2,1)S(1)}, u32[]{:S(2)}, u32[]{:S(2)}) collective-permute-start(bf16[1,128]{1,0:T(2,128)(2,1)S(1)} %get-tuple-element.31), channel_id=1, source_target_pairs={{4,0},{8,4},{12,8},{16,12},{20,16},{24,20},{28,24},{5,1},{9,5},{13... | collective-permute-start | bytes 776 | tf_op jit(solution)/shard_map/ppermute | solution.py:17
  40.4 15.0 %collective-permute-start.2 = (bf16[1,128]{1,0:T(2,128)(2,1)S(1)}, bf16[1,128]{1,0:T(2,128)(2,1)S(1)}, u32[]{:S(2)}, u32[]{:S(2)}) collective-permute-start(bf16[1,128]{1,0:T(2,128)(2,1)S(1)} %get-tuple-element.30), channel_id=1, source_target_pairs={{0,4},{4,8},{8,12},{12,16},{16,20},{20,24},{24,28},{1,5},{5,9},{9,... | collective-permute-start | bytes 776 | tf_op jit(solution)/shard_map/ppermute | solution.py:14
  49.4 12.5 %all-to-all-start.1 = ((bf16[8,4,128]{2,1,0:T(4,128)(2,1)}), bf16[8,4,128]{2,1,0:T(4,128)(2,1)S(1)}, u32[]{:S(2)}, u32[]{:S(2)}) async-start(bf16[8,4,128]{2,1,0:T(4,128)(2,1)} %select_convert_fusion), calls=%async_computation.1 | async-start | bytes 16384 | tf_op jit(solution)/shard_map/all_to_all | solution.py:52
  55.4 39.5 %all-gather.2.cloned.1.call-start = ((), (), s32[]{:S(2)}) async-start(), calls=%async_computation.2 | async-start | bytes 3932160 | tf_op jit(solution)/shard_map/all_gather | solution.py:79
  67.9 111.0 %all-reduce.7.cloned.1.call-start = ((), (), s32[]{:S(2)}) async-start(), calls=%async_computation.3 | async-start | bytes 2097152 | tf_op jit(solution)/shard_map/psum | solution.py:82
  180.3 1.2 copy-start.2
  265.0 50.4 %copy-start.3 = (f32[512,512]{1,0:T(8,128)S(1)}, f32[512,512]{1,0:T(8,128)}, u32[]{:S(2)}) copy-start(f32[512,512]{1,0:T(8,128)} %fusion.13) | copy-start | bytes 3145732
  316.2 1.9 copy-start.1
Sparse Core Ops, SparseCore 0:
  68.1 26.7 all-gather.1
  100.7 78.1 all-reduce.6
where the time goes:
time: 332 us; the launch traced here: 327 us
  other arithmetic  148 us (45%)
  waiting for transfers between devices  107 us (32%)
  starting transfers between devices  25.4 us (8%)
  between operations  18.5 us (6%)
  local copies, waits for them, and re-layouts  15.4 us (5%)
  matrix products  12.6 us (4%)
    another operation x14, other arithmetic, body(): lower_factor = jnp.linalg.cholesky(gram_matrix)  78.7 us
    psum x1, waiting for transfers between devices, body(): gram_matrix = lax.psum(gram_whole, 'rows') / total_rows  77.2 us
    another operation x3, other arithmetic, body(): jax.scipy.linalg.solve_triangular(lower_factor, identity, lower=True)  40.3 us
    all_gather x1, waiting for transfers between devices, body(): columns = lax.all_gather(filtered, 'vecs', axis=1, tiled=True)  26.4 us
    all_to_all x2, starting transfers between devices, apply_operator(): lax.all_to_all(outgoing.astype(jnp.bfloat16), 'rows', split_axis=0, conca...  12.2 us
    ppermute x2, starting transfers between devices, with_halo(): lax.ppermute(lax.slice_in_dim(block, block.shape[dim] - width, None, axis...  10.1 us
    another operation x12, local copies, waits for them, and re-layouts  9.73 us
  transfers between devices with their start and end apart: 8, of which 3 were waited for; matrix products, arithmetic and copies ran while one was open for 5% of the time, Pallas kernels for 0%

commit v1 on v0

--- a/solution.py
+++ b/solution.py
@@ -79,7 +79,7 @@
     columns = lax.all_gather(filtered, "vecs", axis=1, tiled=True)
     total_rows = filtered.shape[0] * part_count
     gram_whole = jnp.einsum("rb,rc->bc", columns, columns, preferred_element_type=jnp.float32)
-    gram_matrix = lax.psum(gram_whole, "rows") / total_rows
+    gram_matrix = jnp.sum(lax.all_gather(gram_whole, "rows"), axis=0) / total_rows
     lower_factor = jnp.linalg.cholesky(gram_matrix)
     identity = jnp.eye(gram_matrix.shape[0], dtype=jnp.float32)
     inverse = jax.scipy.linalg.solve_triangular(lower_factor, identity, lower=True)

time: 332 us -> 382 us (1.15)
  waiting for transfers between devices: 107 us -> 153 us
  other arithmetic: 148 us -> 152 us
    all_gather x0 -> x1, waiting for transfers between devices: none -> 123 us  [body(): lax.all_gather(gram_whole, 'rows')]
    psum x1 -> x0, waiting for transfers between devices: 77.2 us -> none  [body(): gram_matrix = lax.psum(gram_whole, 'rows') / total_rows]
    reduce_sum x0 -> x1, other arithmetic: none -> 4.49 us  [body(): jnp.sum(lax.all_gather(gram_whole, 'rows'), axis=0) / total_rows]
  transfers between devices with their start and end apart: 8 -> 8, of which waited for: 3 -> 3; matrix products, arithmetic and copies ran while one was open for 5% -> 4% of each run, Pallas kernels for 0% -> 0%
where the time goes in v1:
time: 382 us; the launch traced here: 378 us
  waiting for transfers between devices  153 us (40%)
  other arithmetic  152 us (40%)
  starting transfers between devices  25.5 us (7%)
  between operations  18.7 us (5%)
  local copies, waits for them, and re-layouts  15.9 us (4%)
  matrix products  12.8 us (3%)
    all_gather x1, waiting for transfers between devices, body(): lax.all_gather(gram_whole, 'rows')  123 us
    another operation x14, other arithmetic, body(): lower_factor = jnp.linalg.cholesky(gram_matrix)  78.8 us
    another operation x3, other arithmetic, body(): jax.scipy.linalg.solve_triangular(lower_factor, identity, lower=True)  40.3 us
    all_gather x1, waiting for transfers between devices, body(): columns = lax.all_gather(filtered, 'vecs', axis=1, tiled=True)  26.4 us
    all_to_all x2, starting transfers between devices, apply_operator(): lax.all_to_all(outgoing.astype(jnp.bfloat16), 'rows', split_axis=0, conca...  13.6 us
    another operation x12, local copies, waits for them, and re-layouts  10.8 us
    ppermute x2, starting transfers between devices, with_halo(): lax.ppermute(lax.slice_in_dim(block, block.shape[dim] - width, None, axis...  8.8 us
  transfers between devices with their start and end apart: 8, of which 3 were waited for; matrix products, arithmetic and copies ran while one was open for 4% of the time, Pallas kernels for 0%

profile of v1, /device:TPU:0, one launch (start us, length us, event | category | flops | bytes accessed | tf_op | source)
XLA Modules:
  0.0 377.8 jit_solution(12636417391464473819)
XLA Ops:
  6.5 0.7 fusion.50
  7.3 4.9 %collective-permute-start = (bf16[1,128]{1,0:T(2,128)(2,1)S(1)}, bf16[1,128]{1,0:T(2,128)(2,1)S(1)}, u32[]{:S(2)}, u32[]{:S(2)}) collective-permute-start(bf16[1,128]{1,0:T(2,128)(2,1)S(1)} %get-tuple-element.32), channel_id=1, source_target_pairs={{0,4},{4,8},{8,12},{12,16},{16,20},{20,24},{24,28},{1,5},{5,9},{9,... | collective-permute-start | bytes 776 | tf_op jit(solution)/shard_map/ppermute | solution.py:14
  12.2 1.3 collective-permute-start.1
  13.5 1.2 convert_element_type.44
  15.0 0.6 gather_fusion
  15.6 0.7 select_convert_fusion.1
  16.3 7.0 %all-to-all-start = ((bf16[8,4,128]{2,1,0:T(4,128)(2,1)}), bf16[8,4,128]{2,1,0:T(4,128)(2,1)S(1)}, u32[]{:S(2)}, u32[]{:S(2)}) async-start(bf16[8,4,128]{2,1,0:T(4,128)(2,1)} %select_convert_fusion.1), calls=%async_computation | async-start | bytes 16384 | tf_op jit(solution)/shard_map/all_to_all | solution.py:52
  25.7 0.4 fusion.1
  26.1 1.1 pad_subtract_fusion.1
  27.7 2.9 maximum_add_fusion
  30.7 3.3 scatter_fusion
  34.0 2.5 fusion.47
  36.6 1.4 fusion
  37.9 0.6 gather_fusion.1
  38.5 0.7 fusion.49
  39.2 3.9 %collective-permute-start.2 = (bf16[1,128]{1,0:T(2,128)(2,1)S(1)}, bf16[1,128]{1,0:T(2,128)(2,1)S(1)}, u32[]{:S(2)}, u32[]{:S(2)}) collective-permute-start(bf16[1,128]{1,0:T(2,128)(2,1)S(1)} %get-tuple-element.30), channel_id=1, source_target_pairs={{0,4},{4,8},{8,12},{12,16},{16,20},{20,24},{24,28},{1,5},{5,9},{9,... | collective-permute-start | bytes 776 | tf_op jit(solution)/shard_map/ppermute | solution.py:14
  43.1 1.3 collective-permute-start.3
  44.4 2.8 pad_subtract_fusion
  47.2 0.7 select_convert_fusion
  47.9 0.9 slice.253
  48.8 6.6 %all-to-all-start.1 = ((bf16[8,4,128]{2,1,0:T(4,128)(2,1)}), bf16[8,4,128]{2,1,0:T(4,128)(2,1)S(1)}, u32[]{:S(2)}, u32[]{:S(2)}) async-start(bf16[8,4,128]{2,1,0:T(4,128)(2,1)} %select_convert_fusion), calls=%async_computation.1 | async-start | bytes 16384 | tf_op jit(solution)/shard_map/all_to_all | solution.py:52
  55.6 2.9 maximum_add_fusion.1
  58.5 3.5 all-to-all-done.1
  62.1 3.3 scatter_fusion.1
  65.3 2.6 subtract_convert_fusion
  68.0 0.5 all-gather.6.cloned.1.call-start
  68.5 26.4 %all-gather.4.cloned.1.call-done = bf16[3072,512]{1,0:T(8,128)(2,1)} async-done(((bf16[3072,128]{1,0:T(8,128)(2,1)}), bf16[3072,512]{1,0:T(8,128)(2,1)}) %all-gather.4.cloned.1.call-update) | async-done | bytes 3145744 | tf_op jit(solution)/shard_map/all_gather | solution.py:79
  94.9 5.8 %fusion.54 = f32[512,512]{1,0:T(8,128)} fusion(bf16[3072,512]{1,0:T(8,128)(2,1)} %all-gather.4.cloned.1.call-done), kind=kOutput, calls=%fused_computation.131 | convolution fusion | flops 1610612736 | bytes 4194304 | tf_op jit(solution)/shard_map/rb,rc->bc/dot_general | solution.py:81
  100.9 1.1 fusion.13
  102.0 123.4 %all-gather.6.cloned.1.call-done = f32[4096,512]{1,0:T(8,128)} async-done(((f32[512,512]{1,0:T(8,128)}), f32[4096,512]{1,0:T(8,128)}) %all-gather.6.cloned.1.call-update) | async-done | bytes 8388624 | tf_op jit(solution)/shard_map/all_gather | solution.py:82
  225.4 4.5 %reduce_sum.9 = f32[512,512]{1,0:T(8,128)S(1)} reduce(f32[8,512,512]{2,1,0:T(8,128)} %bitcast.71, f32[]{:T(128)} %constant.175.clone.1), dimensions={0}, to_apply=%region_4.6 | reduce | flops 1835008 | bytes 9437188 | tf_op jit(solution)/shard_map/reduce_sum | solution.py:82
  229.9 0.3 copy.38
  230.4 0.3 copy.39
  231.0 11.7 %cholesky.104 = f32[128,128]{1,0:T(8,128)S(1)} custom-call(f32[128,128]{1,0:T(8,128)S(1)} %cholesky.266), custom_call_target="Cholesky" | custom-call | tf_op jit(solution)/shard_map/jit(cholesky)/cholesky | solution.py:83
  242.9 9.8 %custom-call.31 = f32[1,128,128]{1,2,0:T(8,128)S(1)} custom-call(f32[1,128,128]{2,1,0:T(8,128)S(1)} %get-tuple-element.43), custom_call_target="InvertDiagBlocksLowerTriangular" | custom-call | tf_op jit(solution)/shard_map/jit(cholesky)/cholesky | solution.py:83
  253.0 0.3 convolution_subtract_fusion.3
  253.3 11.9 %cholesky.217 = f32[128,128]{1,0:T(8,128)S(1)} custom-call(f32[128,128]{1,0:T(8,128)S(1)} %cholesky.270), custom_call_target="Cholesky" | custom-call | tf_op jit(solution)/shard_map/jit(cholesky)/cholesky | solution.py:83
  265.2 9.8 %custom-call.32 = f32[1,128,128]{1,2,0:T(8,128)S(1)} custom-call(f32[1,128,128]{2,1,0:T(8,128)S(1)} %get-tuple-element.40), custom_call_target="InvertDiagBlocksLowerTriangular" | custom-call | tf_op jit(solution)/shard_map/jit(cholesky)/cholesky | solution.py:83
  275.3 0.4 convolution_subtract_fusion.4
  275.7 11.7 %cholesky.238 = f32[128,128]{1,0:T(8,128)S(1)} custom-call(f32[128,128]{1,0:T(8,128)S(1)} %cholesky.275), custom_call_target="Cholesky" | custom-call | tf_op jit(solution)/shard_map/jit(cholesky)/cholesky | solution.py:83
  287.5 0.7 compare_reduce_fusion.2
  288.2 9.8 %custom-call.33 = f32[1,128,128]{1,2,0:T(8,128)S(1)} custom-call(f32[1,128,128]{2,1,0:T(8,128)S(1)} %get-tuple-element.37), custom_call_target="InvertDiagBlocksLowerTriangular" | custom-call | tf_op jit(solution)/shard_map/jit(cholesky)/cholesky | solution.py:83
  298.2 0.4 convolution_subtract_fusion.5
  298.6 11.9 %cholesky.255 = f32[128,128]{1,0:T(8,128)S(1)} custom-call(f32[128,128]{1,0:T(8,128)S(1)} %convolution_subtract_fusion.5), custom_call_target="Cholesky" | custom-call | tf_op jit(solution)/shard_map/jit(cholesky)/cholesky | solution.py:83
  310.5 0.7 compare_reduce_fusion.1
  311.2 0.7 compare_reduce_fusion.3
  314.6 10.8 %while.1 = (s32[]{:T(128)}, f32[512,512]{1,0:T(8,128)S(1)}, s32[4,2]{0,1:T(2,128)S(1)}, f32[4,128,128]{2,1,0:T(8,128)}, s32[]{:T(128)}) while((s32[]{:T(128)}, f32[512,512]{1,0:T(8,128)S(1)}, s32[4,2]{0,1:T(2,128)S(1)}, f32[4,128,128]{2,1,0:T(8,128)}, s32[]{:T(128)}) %tuple.36), condition=%wide.while_cond, body=%wide.while_body.sunk | while | flops 2 | bytes 132705 | solution.py:85
  314.7 0.6 fusion.64
  315.3 2.0 bitcast_dynamic-update-slice_fusion.2
  317.4 0.6 fusion.64
  318.0 2.0 bitcast_dynamic-update-slice_fusion.2
  320.1 0.6 fusion.64
  320.7 2.0 bitcast_dynamic-update-slice_fusion.2
  322.8 0.6 fusion.64
  323.4 2.0 bitcast_dynamic-update-slice_fusion.2
  325.4 40.1 %custom-call.34 = f32[4,128,128]{1,2,0:T(8,128)S(1)} custom-call(f32[4,128,128]{2,1,0:T(8,128)} %get-tuple-element.13), custom_call_target="InvertDiagBlocksLowerTriangular" | custom-call | tf_op jit(solution)/shard_map/jit(_solve_triangular)/triangular_solve | solution.py:85
  365.6 0.3 fusion.51
  365.9 0.4 convolution_subtract_fusion.1
  366.3 0.4 fusion.52
  366.7 0.4 convolution_subtract_fusion
  367.1 0.4 fusion.53
  367.6 0.6 convolution_subtract_fusion.2
  368.2 0.4 convolution_convert_fusion.1
  368.7 2.1 convolution_convert_fusion
  (70 shorter events, 3.5 us)
Async XLA Ops:
  6.5 8.2 %copy-start.4 = (s32[1,8,4]{1,2,0:T(4,128)S(1)}, s32[1,8,4]{1,2,0:T(4,128)}, u32[]{:S(2)}) copy-start(s32[1,8,4]{1,2,0:T(4,128)} %param.16) | copy-start | bytes 388
  7.3 20.1 %collective-permute-start = (bf16[1,128]{1,0:T(2,128)(2,1)S(1)}, bf16[1,128]{1,0:T(2,128)(2,1)S(1)}, u32[]{:S(2)}, u32[]{:S(2)}) collective-permute-start(bf16[1,128]{1,0:T(2,128)(2,1)S(1)} %get-tuple-element.32), channel_id=1, source_target_pairs={{0,4},{4,8},{8,12},{12,16},{16,20},{20,24},{24,28},{1,5},{5,9},{9,... | collective-permute-start | bytes 776 | tf_op jit(solution)/shard_map/ppermute | solution.py:14
  12.1 13.2 %copy-start.7 = (s32[1,4]{1,0:T(1,128)S(1)}, s32[1,4]{1,0:T(1,128)}, u32[]{:S(2)}) copy-start(s32[1,4]{1,0:T(1,128)} %param.14) | copy-start | bytes 52
  12.2 13.5 %copy-start.5 = (f32[3072]{0:T(1024)S(1)}, f32[3072]{0:T(1024)}, u32[]{:S(2)}) copy-start(f32[3072]{0:T(1024)} %param.13) | copy-start | bytes 36868
  12.2 15.2 %collective-permute-start.1 = (bf16[1,128]{1,0:T(2,128)(2,1)S(1)}, bf16[1,128]{1,0:T(2,128)(2,1)S(1)}, u32[]{:S(2)}, u32[]{:S(2)}) collective-permute-start(bf16[1,128]{1,0:T(2,128)(2,1)S(1)} %get-tuple-element.33), channel_id=1, source_target_pairs={{4,0},{8,4},{12,8},{16,12},{20,16},{24,20},{28,24},{5,1},{9,5},{13... | collective-permute-start | bytes 776 | tf_op jit(solution)/shard_map/ppermute | solution.py:17
  16.3 14.3 %all-to-all-start = ((bf16[8,4,128]{2,1,0:T(4,128)(2,1)}), bf16[8,4,128]{2,1,0:T(4,128)(2,1)S(1)}, u32[]{:S(2)}, u32[]{:S(2)}) async-start(bf16[8,4,128]{2,1,0:T(4,128)(2,1)} %select_convert_fusion.1), calls=%async_computation | async-start | bytes 16384 | tf_op jit(solution)/shard_map/all_to_all | solution.py:52
  26.0 1.3 copy-start.6
  26.1 1.3 slice-start
  26.1 1.6 copy-start
  26.1 1.6 copy-start.3
  39.2 16.3 %collective-permute-start.2 = (bf16[1,128]{1,0:T(2,128)(2,1)S(1)}, bf16[1,128]{1,0:T(2,128)(2,1)S(1)}, u32[]{:S(2)}, u32[]{:S(2)}) collective-permute-start(bf16[1,128]{1,0:T(2,128)(2,1)S(1)} %get-tuple-element.30), channel_id=1, source_target_pairs={{0,4},{4,8},{8,12},{12,16},{16,20},{20,24},{24,28},{1,5},{5,9},{9,... | collective-permute-start | bytes 776 | tf_op jit(solution)/shard_map/ppermute | solution.py:14
  43.1 12.4 %collective-permute-start.3 = (bf16[1,128]{1,0:T(2,128)(2,1)S(1)}, bf16[1,128]{1,0:T(2,128)(2,1)S(1)}, u32[]{:S(2)}, u32[]{:S(2)}) collective-permute-start(bf16[1,128]{1,0:T(2,128)(2,1)S(1)} %get-tuple-element.31), channel_id=1, source_target_pairs={{4,0},{8,4},{12,8},{16,12},{20,16},{24,20},{28,24},{5,1},{9,5},{13... | collective-permute-start | bytes 776 | tf_op jit(solution)/shard_map/ppermute | solution.py:17
  48.8 13.2 %all-to-all-start.1 = ((bf16[8,4,128]{2,1,0:T(4,128)(2,1)}), bf16[8,4,128]{2,1,0:T(4,128)(2,1)S(1)}, u32[]{:S(2)}, u32[]{:S(2)}) async-start(bf16[8,4,128]{2,1,0:T(4,128)(2,1)} %select_convert_fusion), calls=%async_computation.1 | async-start | bytes 16384 | tf_op jit(solution)/shard_map/all_to_all | solution.py:52
  55.4 39.5 %all-gather.4.cloned.1.call-start = ((), (), s32[]{:S(2)}) async-start(), calls=%async_computation.2 | async-start | bytes 3932160 | tf_op jit(solution)/shard_map/all_gather | solution.py:79
  68.0 157.4 %all-gather.6.cloned.1.call-start = ((), (), s32[]{:S(2)}) async-start(), calls=%async_computation.3 | async-start | bytes 9437184 | tf_op jit(solution)/shard_map/all_gather | solution.py:82
  314.5 51.4 %copy-start.2 = (f32[512,512]{1,0:T(8,128)S(1)}, f32[512,512]{1,0:T(8,128)}, u32[]{:S(2)}) copy-start(f32[512,512]{1,0:T(8,128)} %fusion.13) | copy-start | bytes 3145732
  366.7 1.9 copy-start.1
Sparse Core Ops, SparseCore 0:
  68.1 26.7 all-gather.3
  100.9 124.4 all-gather.5
